TPU v7x, 32 devices: a whole 2x2x4 slice. The times are simulated.
32 devices in a mesh: dp: 2 (over x), expert: 16 (over z, y, core).
Axes of the slice: x: 2, y: 2, z: 4, core: 2. Of those that a mesh axis runs over, the one named last changes fastest.
Arguments:
- out_grad: bfloat16 [4096, 1040], P(('dp', 'expert')), may hold values from -8 to 8
- routes: int32 [4096, 1], P(('dp', 'expert')), may hold values from 0 to 15; in each aligned block of 128 rows (0 to 127, 128 to 255, ...) at most 12 rows name the same one
- pre_act: bfloat16 [6144, 3072], P(('dp', 'expert')), may hold values from -6 to 6
- out_weight: bfloat16 [16, 3072, 1040], P('expert', 'dp'), may hold values from -0.109375 to 0.109375
- row_factor: float32 [16, 3072], P('expert', 'dp'), may hold values from 1 to 100
- col_factor: float32 [16, 1040], P('expert'), may hold values from 1 to 100
Outputs:
- hidden_grad: bfloat16 [4096, 3072], P(('dp', 'expert'))
- new_weight: bfloat16 [16, 3072, 1040], P('expert', 'dp')
- new_row: float32 [16, 3072], P('expert', 'dp')
- new_col: float32 [16, 1040], P('expert')
Inputs may be any that keep to these rules, and one draw needn't show every extreme that they name: `routes`: in the rows of one device no expert is named by more than 12 rows.
All inputs are finite; a program needn't handle non-finite values.
Results may differ from a plain program's by a relative error of at most 0.0025.
Values may be sent and summed in bfloat16 or wider, within the bound.
A program may use at most 64 MiB of HBM per device.

v0:
```python
import jax
import jax.numpy as jnp
from jax import lax
from jax.sharding import PartitionSpec as P


def shards(out_grad, routes, pre_act, out_weight, row_factor, col_factor):
    tok_rows = out_grad.shape[0]
    slot_rows = pre_act.shape[0]
    per_expert = slot_rows // lax.axis_size("expert")
    target = routes[:, 0]
    same = target[:, None] == target[None, :]
    earlier = jnp.arange(tok_rows)[None, :] < jnp.arange(tok_rows)[:, None]
    order_in = jnp.sum((same & earlier).astype(jnp.int32), axis=1)
    slots = target * per_expert + order_in
    placing = (slots[None, :] == jnp.arange(slot_rows, dtype=jnp.int32)[:, None]).astype(
        jnp.bfloat16
    )
    outgoing = jnp.dot(placing, out_grad, preferred_element_type=jnp.float32).astype(jnp.bfloat16)
    arrived = lax.all_to_all(outgoing, "expert", split_axis=0, concat_axis=0, tiled=True)
    pre_cols = lax.all_to_all(pre_act, "dp", split_axis=1, concat_axis=0, tiled=True)
    hidden = jnp.maximum(pre_cols, 0)
    weight = out_weight[0]
    piece = lax.all_gather(arrived, "dp", axis=0, tiled=True)
    grad_sum = lax.dot_general(
        hidden, piece, (((0,), (0,)), ((), ())), preferred_element_type=jnp.float32
    )
    back_part = lax.dot_general(
        piece, weight, (((1,), (1,)), ((), ())), preferred_element_type=jnp.float32
    )
    back_cols = jnp.where(pre_cols > 0, back_part, 0.0).astype(jnp.bfloat16)
    back_rows = lax.all_to_all(back_cols, "dp", split_axis=0, concat_axis=1, tiled=True)
    returned = lax.all_to_all(back_rows, "expert", split_axis=0, concat_axis=0, tiled=True)
    hidden_grad = lax.dot_general(
        placing, returned, (((0,), (0,)), ((), ())), preferred_element_type=jnp.float32
    ).astype(jnp.bfloat16)
    full_rows = grad_sum.shape[0] * lax.axis_size("dp")
    width = grad_sum.shape[1]
    squares = grad_sum * grad_sum + 1e-30
    row_new = 0.8 * row_factor[0] + 0.2 * jnp.mean(squares, axis=1)
    col_total = lax.psum(jnp.sum(squares, axis=0), "dp")
    col_new = 0.8 * col_factor[0] + 0.2 * col_total / full_rows
    second = row_new[:, None] * col_new[None, :]
    update = grad_sum * lax.rsqrt(second)
    total_sq = lax.psum(jnp.sum(update * update), "dp")
    spread = jnp.sqrt(total_sq / (full_rows * width))
    update = update / jnp.maximum(1.0, spread / 0.01)
    weight_new = (weight.astype(jnp.float32) - update).astype(jnp.bfloat16)
    return (hidden_grad, weight_new[None], row_new[None], col_new[None])


def solution(mesh):
    placed = (
        P(("dp", "expert"), None),
        P(("dp", "expert"), None),
        P(("dp", "expert"), None),
        P("expert", "dp", None),
        P("expert", "dp"),
        P("expert", None),
    )
    return jax.shard_map(
        shards,
        mesh=mesh,
        in_specs=placed,
        out_specs=(
            P(("dp", "expert"), None),
            P("expert", "dp", None),
            P("expert", "dp"),
            P("expert", None),
        ),
        check_vma=False,
    )
```

profile of v0, /device:TPU:13, one launch (start us, length us, event | category | flops | bytes accessed | tf_op | source)
XLA Modules:
  0.0 138.7 jit_solution(13556714505763052644)
XLA Ops:
  0.7 2.4 %copy.19 = bf16[24,2,8,1536]{3,2,0,1:T(8,128)(2,1)} copy(bf16[24,2,8,1536]{3,2,1,0:T(8,128)(2,1)} %bitcast.32) | data formatting | bytes 2359296 | tf_op jit(solution)/shard_map/all_to_all | solution.py:21
  3.1 3.6 %all-to-all-start = ((bf16[192,2,1536]{2,0,1:T(8,128)(2,1)}), bf16[192,2,1536]{2,0,1:T(8,128)(2,1)S(1)}, u32[]{:S(2)}, u32[]{:S(2)}) async-start(bf16[192,2,1536]{2,0,1:T(8,128)(2,1)} %bitcast.30), calls=%async_computation | async-start | bytes 2359296 | tf_op jit(solution)/shard_map/all_to_all | solution.py:21
  6.9 0.3 convolution_convert_fusion.1
  7.2 0.9 all_to_all.40
  8.2 12.9 %all-to-all-done = bf16[192,2,1536]{2,0,1:T(8,128)(2,1)S(1)} async-done(((bf16[192,2,1536]{2,0,1:T(8,128)(2,1)}), bf16[192,2,1536]{2,0,1:T(8,128)(2,1)S(1)}, u32[]{:S(2)}, u32[]{:S(2)}) %all-to-all-start) | async-done | bytes 1179680 | tf_op jit(solution)/shard_map/all_to_all | solution.py:21
  21.1 7.4 %all-to-all-start.1 = ((bf16[16,12,1040]{2,1,0:T(8,128)(2,1)}), bf16[16,12,1040]{2,1,0:T(8,128)(2,1)S(1)}, u32[]{:S(2)}, u32[]{:S(2)}) async-start(bf16[16,12,1040]{2,1,0:T(8,128)(2,1)} %all_to_all.40), calls=%async_computation.1 | async-start | bytes 1179648 | tf_op jit(solution)/shard_map/all_to_all | solution.py:20
  28.5 1.1 broadcast_compare_fusion
  29.7 13.8 %all-to-all-done.1 = bf16[16,12,1040]{2,1,0:T(8,128)(2,1)S(1)} async-done(((bf16[16,12,1040]{2,1,0:T(8,128)(2,1)}), bf16[16,12,1040]{2,1,0:T(8,128)(2,1)S(1)}, u32[]{:S(2)}, u32[]{:S(2)}) %all-to-all-start.1) | async-done | bytes 399392 | tf_op jit(solution)/shard_map/all_to_all | solution.py:20
  43.7 12.3 %all_gather.3 = bf16[384,1040]{1,0:T(8,128)(2,1)S(1)} all-gather(bf16[192,1040]{1,0:T(8,128)(2,1)S(1)} %all_to_all.42), channel_id=1, replica_groups=mesh['dp'=2,'expert'=16] {'dp'}, dimensions={0}, use_global_device_ids=true | all-gather | bytes 1198080 | tf_op jit(solution)/shard_map/all_gather | solution.py:24
  56.0 4.8 %fusion.8 = bf16[384,1536]{1,0:T(8,128)(2,1)} fusion(pred[384,1536]{1,0:T(32,128)(4,1)} %bitcast.34, bf16[384,1040]{1,0:T(8,128)(2,1)S(1)} %all_gather.3, bf16[1,1536,1040]{1,2,0:T(8,128)(2,1)} %param.9), kind=kOutput, calls=%fused_computation.11 | convolution fusion | flops 1228013568 | bytes 5763072 | tf_op jit(solution)/shard_map/dot_general | solution.py:28
  60.7 3.6 %all-to-all-start.2 = ((bf16[2,192,1536]{2,1,0:T(8,128)(2,1)}), bf16[2,192,1536]{2,1,0:T(8,128)(2,1)S(1)}, u32[]{:S(2)}, u32[]{:S(2)}) async-start(bf16[2,192,1536]{2,1,0:T(8,128)(2,1)} %bitcast.4), calls=%async_computation.2 | async-start | bytes 2359296 | tf_op jit(solution)/shard_map/all_to_all | solution.py:32
  64.3 4.8 %fusion.1 = (f32[1536]{0:T(1024)S(1)}, f32[1040]{0:T(1024)S(1)}, f32[1536,1040]{0,1:T(8,128)}) fusion(bf16[384,1536]{1,0:T(8,128)(2,1)S(1)} %bitcast.33, bf16[384,1040]{1,0:T(8,128)(2,1)S(1)} %all_gather.3), kind=kOutput, calls=%fused_computation.5 | convolution fusion | flops 1233221120 | bytes 8378432 | tf_op jit(solution)/shard_map/dot_general | solution.py:25
  69.1 9.5 %psum.14 = f32[1040]{0:T(1024)S(1)} all-reduce(f32[1040]{0:T(1024)S(1)} %get-tuple-element.5), channel_id=1, replica_groups=mesh['dp'=2,'expert'=16] {'dp'}, use_global_device_ids=true, to_apply=%region_3.4 | all-reduce | flops 1040 | bytes 8320 | tf_op jit(solution)/shard_map/psum | solution.py:41
  78.6 5.5 %multiply_reduce_fusion = f32[]{:T(128)} fusion(f32[1536,1040]{0,1:T(8,128)} %get-tuple-element.8, f32[1040]{0:T(1024)S(1)} %multiply_add_fusion.1, f32[1536]{0:T(1024)S(1)} %get-tuple-element.7), kind=kLoop, calls=%fused_computation.1 | loop fusion | flops 6389759 | bytes 6400068 | tf_op jit(solution)/shard_map/reduce_sum | solution.py:45
  84.1 4.4 %psum.15 = f32[]{:T(128)} all-reduce(f32[]{:T(128)} %multiply_reduce_fusion), channel_id=1, replica_groups=mesh['dp'=2,'expert'=16] {'dp'}, use_global_device_ids=true, to_apply=%region_5.6 | all-reduce | flops 1 | bytes 8 | tf_op jit(solution)/shard_map/psum | solution.py:45
  88.5 0.6 broadcast_in_dim.10
  89.8 0.6 reshape_add_fusion
  90.4 1.2 copy.16
  91.6 1.6 %all_to_all.46 = bf16[16,12,3072]{2,1,0:T(8,128)(2,1)} reshape(bf16[192,2,1536]{2,1,0:T(2,128)(2,1)S(1)} %copy.16) | data formatting | bytes 2359296 | tf_op jit(solution)/shard_map/all_to_all | solution.py:33
  93.2 7.7 %all-to-all-start.3 = ((bf16[16,12,3072]{2,1,0:T(8,128)(2,1)}), bf16[16,12,3072]{2,1,0:T(8,128)(2,1)S(1)}, u32[]{:S(2)}, u32[]{:S(2)}) async-start(bf16[16,12,3072]{2,1,0:T(8,128)(2,1)} %all_to_all.46), calls=%async_computation.3 | async-start | bytes 3145728 | tf_op jit(solution)/shard_map/all_to_all | solution.py:33
  100.9 5.8 %fusion.4 = bf16[1,1536,1040]{1,2,0:T(8,128)(2,1)} fusion(f32[]{:T(128)S(6)} %max_shard_map.3, f32[1536,1040]{0,1:T(8,128)} %get-tuple-element.8, f32[1040]{0:T(1024)S(1)} %multiply_add_fusion.1, f32[1536]{0:T(1024)S(1)} %get-tuple-element.7, bf16[1,1536,1040]{1,2,0:T(8,128)(2,1)} %param.9), kind=kLoop, calls=%fused_computation.9 | loop fusion | flops 9584640 | bytes 12789828 | tf_op jit(solution)/shard_map/broadcast_in_dim | solution.py:49
  106.7 30.4 %all-to-all-done.3 = bf16[16,12,3072]{2,1,0:T(8,128)(2,1)S(1)} async-done(((bf16[16,12,3072]{2,1,0:T(8,128)(2,1)}), bf16[16,12,3072]{2,1,0:T(8,128)(2,1)S(1)}, u32[]{:S(2)}, u32[]{:S(2)}) %all-to-all-start.3) | async-done | bytes 1179680 | tf_op jit(solution)/shard_map/all_to_all | solution.py:33
  137.1 0.3 all_to_all.48
  137.4 1.3 convolution_convert_fusion
  (17 shorter events, 0.5 us)
Async XLA Ops:
  0.6 6.3 %copy-start = (bf16[128,1040]{0,1:T(8,128)(2,1)S(1)}, bf16[128,1040]{0,1:T(8,128)(2,1)}, u32[]{:S(2)}) copy-start(bf16[128,1040]{0,1:T(8,128)(2,1)} %param.6) | copy-start | bytes 798724
  0.6 6.0 %copy-start.3 = (s32[128,1]{0,1:T(1,128)S(1)}, s32[128,1]{0,1:T(1,128)}, u32[]{:S(2)}) copy-start(s32[128,1]{0,1:T(1,128)} %param.7) | copy-start | bytes 1540
  0.7 7.5 %copy-start.2 = (f32[1,1040]{1,0:T(1,128)S(1)}, f32[1,1040]{1,0:T(1,128)}, u32[]{:S(2)}) copy-start(f32[1,1040]{1,0:T(1,128)} %param.11) | copy-start | bytes 12484
  0.7 7.5 %copy-start.1 = (f32[1,1536]{1,0:T(1,128)S(1)}, f32[1,1536]{1,0:T(1,128)}, u32[]{:S(2)}) copy-start(f32[1,1536]{1,0:T(1,128)} %param.10) | copy-start | bytes 18436
  3.1 18.0 %all-to-all-start = ((bf16[192,2,1536]{2,0,1:T(8,128)(2,1)}), bf16[192,2,1536]{2,0,1:T(8,128)(2,1)S(1)}, u32[]{:S(2)}, u32[]{:S(2)}) async-start(bf16[192,2,1536]{2,0,1:T(8,128)(2,1)} %bitcast.30), calls=%async_computation | async-start | bytes 2359296 | tf_op jit(solution)/shard_map/all_to_all | solution.py:21
  21.1 22.4 %all-to-all-start.1 = ((bf16[16,12,1040]{2,1,0:T(8,128)(2,1)}), bf16[16,12,1040]{2,1,0:T(8,128)(2,1)S(1)}, u32[]{:S(2)}, u32[]{:S(2)}) async-start(bf16[16,12,1040]{2,1,0:T(8,128)(2,1)} %all_to_all.40), calls=%async_computation.1 | async-start | bytes 1179648 | tf_op jit(solution)/shard_map/all_to_all | solution.py:20
  60.7 29.7 %all-to-all-start.2 = ((bf16[2,192,1536]{2,1,0:T(8,128)(2,1)}), bf16[2,192,1536]{2,1,0:T(8,128)(2,1)S(1)}, u32[]{:S(2)}, u32[]{:S(2)}) async-start(bf16[2,192,1536]{2,1,0:T(8,128)(2,1)} %bitcast.4), calls=%async_computation.2 | async-start | bytes 2359296 | tf_op jit(solution)/shard_map/all_to_all | solution.py:32
  93.2 43.9 %all-to-all-start.3 = ((bf16[16,12,3072]{2,1,0:T(8,128)(2,1)}), bf16[16,12,3072]{2,1,0:T(8,128)(2,1)S(1)}, u32[]{:S(2)}, u32[]{:S(2)}) async-start(bf16[16,12,3072]{2,1,0:T(8,128)(2,1)} %all_to_all.46), calls=%async_computation.3 | async-start | bytes 3145728 | tf_op jit(solution)/shard_map/all_to_all | solution.py:33
where the time goes:
time: 139 us
  waiting for transfers between devices  57.1 us (41%)
  blocking collectives  26.2 us (19%)
  starting transfers between devices  22.3 us (16%)
  other arithmetic  13.3 us (10%)
  matrix products  11.1 us (8%)
  local copies, waits for them, and re-layouts  7.29 us (5%)
  between operations  1.46 us (1%)
    all_to_all x1, waiting for transfers between devices, shards(): lax.all_to_all(back_rows, 'expert', split_axis=0, concat_axis=0, tiled=True)  30.4 us
    all_to_all x1, waiting for transfers between devices, shards(): lax.all_to_all(outgoing, 'expert', split_axis=0, concat_axis=0, tiled=True)  13.8 us
    all_to_all x1, waiting for transfers between devices, shards(): lax.all_to_all(pre_act, 'dp', split_axis=1, concat_axis=0, tiled=True)  12.9 us
    all_gather x1, blocking collectives, shards(): piece = lax.all_gather(arrived, 'dp', axis=0, tiled=True)  12.3 us
    psum x1, blocking collectives, shards(): col_total = lax.psum(jnp.sum(squares, axis=0), 'dp')  9.49 us
    all_to_all x1, starting transfers between devices, shards(): lax.all_to_all(back_rows, 'expert', split_axis=0, concat_axis=0, tiled=True)  7.69 us
    all_to_all x1, starting transfers between devices, shards(): lax.all_to_all(outgoing, 'expert', split_axis=0, concat_axis=0, tiled=True)  7.38 us
    broadcast_in_dim x1, other arithmetic, shards(): return (hidden_grad, weight_new[None], row_new[None], col_new[None])  5.77 us
  transfers between devices with their start and end apart: 4, of which 3 were waited for; matrix products, arithmetic and copies ran while one was open for 14% of the time, Pallas kernels for 0%

commit v1 on v0

v1 whole, which is shorter than its diff:
```python
import functools
import jax
import jax.numpy as jnp
import numpy as np
from jax import lax
from jax.experimental import pallas as pl
from jax.experimental.pallas import tpu as pltpu
from jax.sharding import PartitionSpec as P

MESH = pl.DeviceIdType.MESH
F32, BF16 = jnp.float32, jnp.bfloat16


def up128(n):
    return -(-n // 128) * 128


def dot(a, b, ca=1, cb=0):
    return lax.dot_general(a, b, (((ca,), (cb,)), ((), ())), preferred_element_type=F32)


def onehot(hit):
    return jnp.where(hit, 1.0, 0.0).astype(BF16)


def kernel(cfg, og, rcol, rrow, pre, w, rf, cf, qn, qt,
           hid, neww, newrow, newcol,
           dy_out, dy_all, dyn, pre_all, wv, grad, snd, ret, colst, place, rfcol, rncol,
           loc, outs, dy_s, dy_r, fw_s, fw_r, pre_s, pre_r, rt_s, rt_r, st_s, st_r):
    n_dp, n_e, slot, groups, chunk = cfg
    tok, d = og.shape
    ff = wv.shape[0]
    r = pre.shape[0]
    packed = slot > 8
    half, dp_off, h0 = ff // 2, up128(d), d // 2 // 128 * 128
    hw = d - h0
    g = n_e // groups
    i, e = lax.axis_index("dp"), lax.axis_index("expert")
    total = n_dp * n_e
    flat = i * n_e + e
    others = [lax.rem(i + o, n_dp) for o in range(1, n_dp)]

    barrier = pltpu.get_barrier_semaphore()

    def greet(k, _):
        t = lax.rem(flat + k, total)
        ti = lax.div(t, n_e)
        pl.semaphore_signal(barrier, inc=1, device_id=(ti, t - ti * n_e), device_id_type=MESH)
        return 0

    lax.fori_loop(1, total, greet, 0)

    get_w = pltpu.make_async_copy(w.at[0], wv, loc.at[0])
    cols = lambda t: pl.ds(pl.multiple_of(t * ff, 128), ff)
    get_pre = pltpu.make_async_copy(pre.at[:, cols(i)], pre_all.at[i], loc.at[1])
    get_w.start()
    get_pre.start()

    same = rcol[...] == rrow[...]
    at_row = lax.broadcasted_iota(jnp.int32, (tok, tok), 0)
    at_col = lax.broadcasted_iota(jnp.int32, (tok, tok), 1)
    order = jnp.sum(jnp.where(same & (at_row < at_col), 1.0, 0.0), axis=0, keepdims=True)
    base = rrow[...].astype(F32) * 8.0 + order
    rows = lax.broadcasted_iota(jnp.int32, (n_e * 8, tok), 0).astype(F32)
    place[0] = onehot(rows == jnp.where(order < 8.0, base, -1.0))
    dy_out[:, :, 0:d] = dot(place[0], og[...]).reshape(n_e, 8, d).astype(BF16)
    if packed:
        place[1] = onehot(rows == jnp.where(order >= 8.0, base - 8.0, -1.0))
        place[2] = onehot(rows == jnp.where(order >= 8.0, base - 4.0, -1.0))
        tail = dot(place[1], og[:, 0:hw]) + dot(place[2], og[:, h0:d])
        dy_out[:, :, dp_off:dp_off + hw] = tail.reshape(n_e, 8, hw).astype(BF16)

    def peer(k):
        return lax.rem(e + lax.rem(k + n_e // 2 - 1, n_e - 1) + 1, n_e)

    def send_dy(k):
        t = peer(k)
        return pltpu.make_async_remote_copy(
            src_ref=dy_out.at[t], dst_ref=dy_all.at[i, e], send_sem=dy_s.at[t],
            recv_sem=dy_r.at[e], device_id=(i, t), device_id_type=MESH)

    def send_pre(t):
        return pltpu.make_async_remote_copy(
            src_ref=pre.at[:, cols(t)], dst_ref=pre_all.at[i], send_sem=pre_s.at[t],
            recv_sem=pre_r.at[i], device_id=(t, e), device_id_type=MESH)

    def send_fw(t, q):
        part = pl.ds(q * g, g)
        return pltpu.make_async_remote_copy(
            src_ref=dy_all.at[i, part], dst_ref=dy_all.at[i, part], send_sem=fw_s.at[t, q],
            recv_sem=fw_r.at[i, q], device_id=(t, e), device_id_type=MESH)

    def send_ret(t, j):
        return pltpu.make_async_remote_copy(
            src_ref=snd.at[t, j], dst_ref=ret.at[i, e], send_sem=rt_s.at[t, j],
            recv_sem=rt_r.at[i, e], device_id=(t, j), device_id_type=MESH)

    def send_st(t):
        return pltpu.make_async_remote_copy(
            src_ref=colst.at[i], dst_ref=colst.at[i], send_sem=st_s.at[t],
            recv_sem=st_r.at[i], device_id=(t, e), device_id_type=MESH)

    def loop(n, act):
        def step(k, _):
            act(k)
            return 0
        lax.fori_loop(0, n, step, 0)

    pl.semaphore_wait(barrier, total - 1)
    loop(n_e - 1, lambda k: send_dy(k).start())
    own = pltpu.make_async_copy(dy_out.at[e], dy_all.at[i, e], dy_r.at[e])
    own.start()
    for t in others:
        send_pre(t).start()

    for b in range(ff // 128):
        lane = slice(b * 128, b * 128 + 128)
        rfcol[lane, :] = jnp.broadcast_to(rf[0:1, lane], (128, 128)).T

    for k in range(groups):
        q = lax.rem(lax.div(e, g) + k, groups)
        for m in range(g):
            j = q * g + m
            pltpu.make_async_copy(dy_out.at[0], dy_all.at[i, j], dy_r.at[j]).wait()
        for t in others:
            send_fw(t, q).start()

    def flat_rows(x):
        return x.astype(F32).reshape(x.shape[0] * 8, x.shape[2]).astype(BF16)

    def back(t):
        dy = dot(qn[0], flat_rows(dy_all[t, :, :, 0:d]))
        if packed:
            tail = flat_rows(dy_all[t, :, :, dp_off:dp_off + hw])
            dy = dy + jnp.concatenate([dot(qn[1], tail[:, 0:h0]), dot(qn[2], tail)], axis=1)
        dy = dy.astype(BF16)
        dyn[t] = dy
        tail = None
        for c in range(2 if packed else 1):
            wide = half if packed else ff
            span = slice(c * wide, c * wide + wide)
            bk = dot(dy, wv[span, :], 1, 1)
            keep = pre_all[t, :, span].astype(F32) > 0.0
            bk = jnp.where(keep, bk, 0.0).astype(BF16)
            snd[t, :, :, span] = dot(qt[0], bk).reshape(n_e, 8, wide).astype(BF16)
            if packed:
                part = dot(qt[1 + c], bk)
                tail = part if tail is None else tail + part
        if packed:
            snd[t, :, :, ff:ff + half] = tail.reshape(n_e, 8, half).astype(BF16)

    get_w.wait()
    get_pre.wait()
    back(i)
    loop(n_e - 1, lambda k: send_ret(i, peer(k)).start())
    own_ret = pltpu.make_async_copy(snd.at[i, e], ret.at[i, e], rt_r.at[i, e])
    own_ret.start()

    for t in others:
        for q in range(groups):
            part = pl.ds(q * g, g)
            pltpu.make_async_copy(dy_all.at[i, part], dy_all.at[t, part], fw_r.at[t, q]).wait()
        pltpu.make_async_copy(pre_all.at[i], pre_all.at[t], pre_r.at[t]).wait()
        back(t)
        loop(n_e, lambda k: send_ret(t, lax.rem(e + n_e // 2 + k, n_e)).start())

    def gradient(c, carry):
        col, weighted = carry
        span = pl.ds(pl.multiple_of(c * chunk, 128), chunk)
        acc = None
        for t in range(n_dp):
            hidden = jnp.maximum(pre_all[t, :, span], 0)
            part = dot(hidden, dyn[t], 0, 0)
            acc = part if acc is None else acc + part
        grad[span, :] = acc
        sq = acc * acc
        rn = 0.8 * rfcol[span, 0:1] + 0.2 * (jnp.sum(sq, axis=1, keepdims=True) / d + 1e-30)
        rncol[span, :] = jnp.broadcast_to(rn, (chunk, 128))
        return (col + jnp.sum(sq, axis=0, keepdims=True),
                weighted + jnp.sum(sq * (1.0 / rn), axis=0, keepdims=True))

    zero = jnp.zeros((1, d), F32)
    col, weighted = lax.fori_loop(0, ff // chunk, gradient, (zero, zero))
    colst[i, 0:1, :] = col
    colst[i, 1:2, :] = weighted
    for t in others:
        send_st(t).start()
    for b in range(ff // 128):
        lane = slice(b * 128, b * 128 + 128)
        newrow[0:1, lane] = rncol[lane, :].T[0:1, :]
    for t in others:
        pltpu.make_async_copy(colst.at[i], colst.at[t], st_r.at[t]).wait()
    col, weighted = zero, zero
    for t in range(n_dp):
        col = col + colst[t, 0:1, :]
        weighted = weighted + colst[t, 1:2, :]
    full = ff * n_dp
    cn = 0.8 * cf[...] + 0.2 * (col / full + 1e-30)
    newcol[...] = cn
    spread = jnp.sqrt(jnp.sum(weighted / cn, axis=1, keepdims=True) / (full * d))
    cs = lax.rsqrt(cn) / jnp.maximum(1.0, spread / 0.01)

    def write(c):
        span = pl.ds(pl.multiple_of(c * chunk, 128), chunk)
        return pltpu.make_async_copy(wv.at[span, :], neww.at[0, span, :], outs.at[c])

    def apply(c):
        span = pl.ds(pl.multiple_of(c * chunk, 128), chunk)
        update = grad[span, :] * lax.rsqrt(rncol[span, 0:1]) * cs
        wv[span, :] = (wv[span, :].astype(F32) - update).astype(BF16)
        write(c).start()

    loop(ff // chunk, apply)

    for t in [i] + others:
        loop(n_e, lambda j: pltpu.make_async_copy(
            snd.at[0, 0], ret.at[t, j], rt_r.at[t, j]).wait())
        for c in range(2 if packed else 1):
            wide = half if packed else ff
            got = dot(place[0], flat_rows(ret[t, :, :, c * wide:c * wide + wide]), 0, 0)
            if packed:
                got = got + dot(place[1 + c], flat_rows(ret[t, :, :, ff:ff + half]), 0, 0)
            hid[:, pl.ds(pl.multiple_of(t * ff + c * wide, 128), wide)] = got.astype(BF16)

    loop(n_e - 1, lambda k: send_dy(k).wait_send())
    loop(n_e - 1, lambda k: send_ret(i, peer(k)).wait_send())
    for t in others:
        send_pre(t).wait_send()
        for q in range(groups):
            send_fw(t, q).wait_send()
        loop(n_e, lambda k: send_ret(t, k).wait_send())
        send_st(t).wait_send()
    loop(ff // chunk, lambda c: write(c).wait())


def shards(out_grad, routes, pre_act, out_weight, row_factor, col_factor):
    n_dp, n_e = lax.axis_size("dp"), lax.axis_size("expert")
    tok, d = out_grad.shape
    r = pre_act.shape[0]
    ff = out_weight.shape[1]
    slot = r // n_e
    packed = slot > 8
    assert slot <= 12
    kinds = 3 if packed else 1
    groups = 4
    chunk = next(c for c in (384, 256, 128) if ff % c == 0)
    wide_d = up128(d) + d - d // 2 // 128 * 128 if packed else d
    wide_f = ff + ff // 2 if packed else ff
    row = np.arange(r)
    src, s = row // slot, row % slot
    q = np.zeros((kinds, r, n_e * 8), np.float32)
    low = s < 8
    q[0, row[low], (src * 8 + s)[low]] = 1
    if packed:
        q[1, row[~low], (src * 8 + s - 8)[~low]] = 1
        q[2, row[~low], (src * 8 + s - 4)[~low]] = 1
    qn = jnp.asarray(q, BF16)
    qt = jnp.asarray(q.transpose(0, 2, 1), BF16)
    vm = pl.BlockSpec(memory_space=pltpu.VMEM)
    hbm = pl.BlockSpec(memory_space=pl.ANY)
    dma = pltpu.SemaphoreType.DMA
    sds = jax.ShapeDtypeStruct
    return pl.pallas_call(
        functools.partial(kernel, (n_dp, n_e, slot, groups, chunk)),
        out_shape=(sds((tok, ff * n_dp), BF16), sds((1, ff, d), BF16),
                   sds((1, ff), F32), sds((1, d), F32)),
        in_specs=[vm, vm, vm, hbm, hbm, vm, vm, vm, vm],
        out_specs=(vm, hbm, vm, vm),
        scratch_shapes=[
            pltpu.VMEM((n_e, 8, wide_d), BF16),
            pltpu.VMEM((n_dp, n_e, 8, wide_d), BF16),
            pltpu.VMEM((n_dp, r, d), BF16),
            pltpu.VMEM((n_dp, r, ff), BF16),
            pltpu.VMEM((ff, d), BF16),
            pltpu.VMEM((ff, d), F32),
            pltpu.VMEM((n_dp, n_e, 8, wide_f), BF16),
            pltpu.VMEM((n_dp, n_e, 8, wide_f), BF16),
            pltpu.VMEM((n_dp, 2, d), F32),
            pltpu.VMEM((kinds, n_e * 8, tok), BF16),
            pltpu.VMEM((ff, 128), F32),
            pltpu.VMEM((ff, 128), F32),
            dma((2,)), dma((ff // chunk,)), dma((n_e,)), dma((n_e,)),
            dma((n_dp, groups)), dma((n_dp, groups)), dma((n_dp,)), dma((n_dp,)),
            dma((n_dp, n_e)), dma((n_dp, n_e)), dma((n_dp,)), dma((n_dp,)),
        ],
        compiler_params=pltpu.CompilerParams(
            collective_id=0, has_side_effects=True, vmem_limit_bytes=60 * 1024 * 1024),
    )(out_grad, routes, routes.reshape(1, tok), pre_act, out_weight, row_factor, col_factor, qn, qt)


def solution(mesh):
    placed = (
        P(("dp", "expert"), None),
        P(("dp", "expert"), None),
        P(("dp", "expert"), None),
        P("expert", "dp", None),
        P("expert", "dp"),
        P("expert", None),
    )
    return jax.shard_map(
        shards,
        mesh=mesh,
        in_specs=placed,
        out_specs=(
            P(("dp", "expert"), None),
            P("expert", "dp", None),
            P("expert", "dp"),
            P("expert", None),
        ),
        check_vma=False,
    )
```

time: 139 us -> 71.8 us (0.52)
  the two profiles are of different devices: /device:TPU:13 before, /device:TPU:0 now
where the time goes in v1:
time: 71.8 us; the launch traced here: 71.4 us
  Pallas kernels  54.3 us (76%)
  local copies, waits for them, and re-layouts  16.4 us (23%)
    pallas_call x1, Pallas kernels, shards(): pl.pallas_call(functools.partial(kernel, (n_dp, n_e, slot, groups, chunk)...  54.3 us
    unnamed x12, local copies, waits for them, and re-layouts  10.7 us
    pallas_call x1, local copies, waits for them, and re-layouts, shards(): pl.pallas_call(functools.partial(kernel, (n_dp, n_e, slot, groups, chunk)...  5.7 us

profile of v1, /device:TPU:0, one launch (start us, length us, event | category | flops | bytes accessed | tf_op | source)
XLA Modules:
  0.0 71.4 jit_solution(7903408668737882511)
XLA Ops:
  0.6 1.4 %copy.13.rcol = s32[128,1]{1,0:T(8,128)} copy(s32[128,1]{0,1:T(1,128)} %param.9) | data formatting | bytes 1024 | tf_op args[1]
  2.0 1.8 %copy.12.og = bf16[128,1040]{1,0:T(8,128)(2,1)} copy(bf16[128,1040]{0,1:T(8,128)(2,1)} %param.8) | data formatting | bytes 532480 | tf_op args[0]
  3.9 5.4 %copy.14.w = bf16[1,1536,1040]{2,1,0:T(8,128)(2,1)} copy(bf16[1,1536,1040]{1,2,0:T(8,128)(2,1)} %param.11) | data formatting | bytes 6389760 | tf_op args[3]
  9.3 54.3 %shard_map.111 = (bf16[128,3072]{1,0:T(8,128)(2,1)}, bf16[1,1536,1040]{2,1,0:T(8,128)(2,1)}, f32[1,1536]{1,0:T(1,128)}, f32[1,1040]{1,0:T(1,128)}) custom-call(bf16[128,1040]{1,0:T(8,128)(2,1)} %copy.12.og, s32[128,1]{1,0:T(8,128)} %copy.13.rcol, s32[1,128]{1,0:T(1,128)} %bitcast.1, bf16[192,3072]{1,0:T(8,128)(2,1)} %pre.1, bf16[1,1536,1040]{2,1,0:T(8,128)(2,1)} %copy.14.w, ...), custom_call_target="tpu_custom_call" | custom-call | tf_op jit(solution)/shard_map/pallas_call | solution.py:263
  63.6 0.0 copy-start
  63.6 0.0 copy-start.1
  63.6 0.0 copy-start.2
  63.6 5.7 %copy.15 = bf16[1,1536,1040]{1,2,0:T(8,128)(2,1)} copy(bf16[1,1536,1040]{2,1,0:T(8,128)(2,1)} %get-tuple-element.5) | data formatting | bytes 6389760 | tf_op jit(solution)/shard_map/pallas_call | solution.py:263
  69.3 0.0 copy-done
  69.3 0.9 %copy.19 = bf16[128,3072]{1,0:T(8,128)(2,1)} copy(bf16[128,3072]{1,0:T(8,128)(2,1)S(1)} %copy-done) | data formatting | bytes 1572864
  70.2 0.0 copy-done.1
  70.2 0.6 copy.20
  70.8 0.0 copy-done.2
  70.8 0.6 copy.21
Async XLA Ops:
  63.6 5.7 %copy-start = (bf16[128,3072]{1,0:T(8,128)(2,1)S(1)}, bf16[128,3072]{1,0:T(8,128)(2,1)}, u32[]{:S(2)}) copy-start(bf16[128,3072]{1,0:T(8,128)(2,1)} %get-tuple-element.12) | copy-start | bytes 2359300
  63.6 6.6 %copy-start.1 = (f32[1,1536]{1,0:T(1,128)S(1)}, f32[1,1536]{1,0:T(1,128)}, u32[]{:S(2)}) copy-start(f32[1,1536]{1,0:T(1,128)} %get-tuple-element.14) | copy-start | bytes 18436
  63.6 7.2 %copy-start.2 = (f32[1,1040]{1,0:T(1,128)S(1)}, f32[1,1040]{1,0:T(1,128)}, u32[]{:S(2)}) copy-start(f32[1,1040]{1,0:T(1,128)} %get-tuple-element.15) | copy-start | bytes 12484

commit v2 on v1

--- a/solution.py
+++ b/solution.py
@@ -23,13 +23,13 @@
     return jnp.where(hit, 1.0, 0.0).astype(BF16)
 
 
-def kernel(cfg, og, rcol, rrow, pre, w, rf, cf, qn, qt,
+def kernel(cfg, og, rrow, pre, w, rf, cf, qn, qt,
            hid, neww, newrow, newcol,
-           dy_out, dy_all, dyn, pre_all, wv, grad, snd, ret, colst, place, rfcol, rncol,
-           loc, outs, dy_s, dy_r, fw_s, fw_r, pre_s, pre_r, rt_s, rt_r, st_s, st_r):
-    n_dp, n_e, slot, groups, chunk = cfg
-    tok, d = og.shape
-    ff = wv.shape[0]
+           dy_out, dy_all, dyn, pre_all, wv, grad, snd, ret, colst, place, colacc, cspad, cscol,
+           loc, dy_s, dy_r, fw_s, fw_r, pre_s, pre_r, rt_s, rt_r, st_s, st_r):
+    n_dp, n_e, slot, groups, chunk, deep = cfg
+    d, tok = og.shape
+    ff = wv.shape[1]
     r = pre.shape[0]
     packed = slot > 8
     half, dp_off, h0 = ff // 2, up128(d), d // 2 // 128 * 128
@@ -56,18 +56,19 @@
     get_w.start()
     get_pre.start()
 
-    same = rcol[...] == rrow[...]
+    named = jnp.broadcast_to(rrow[...].astype(F32), (tok, tok))
+    same = named == named.T
     at_row = lax.broadcasted_iota(jnp.int32, (tok, tok), 0)
     at_col = lax.broadcasted_iota(jnp.int32, (tok, tok), 1)
     order = jnp.sum(jnp.where(same & (at_row < at_col), 1.0, 0.0), axis=0, keepdims=True)
     base = rrow[...].astype(F32) * 8.0 + order
     rows = lax.broadcasted_iota(jnp.int32, (n_e * 8, tok), 0).astype(F32)
     place[0] = onehot(rows == jnp.where(order < 8.0, base, -1.0))
-    dy_out[:, :, 0:d] = dot(place[0], og[...]).reshape(n_e, 8, d).astype(BF16)
+    dy_out[:, :, 0:d] = dot(place[0], og[...], 1, 1).reshape(n_e, 8, d).astype(BF16)
     if packed:
         place[1] = onehot(rows == jnp.where(order >= 8.0, base - 8.0, -1.0))
         place[2] = onehot(rows == jnp.where(order >= 8.0, base - 4.0, -1.0))
-        tail = dot(place[1], og[:, 0:hw]) + dot(place[2], og[:, h0:d])
+        tail = dot(place[1], og[0:hw, :], 1, 1) + dot(place[2], og[h0:d, :], 1, 1)
         dy_out[:, :, dp_off:dp_off + hw] = tail.reshape(n_e, 8, hw).astype(BF16)
 
     def peer(k):
@@ -113,9 +114,7 @@
     for t in others:
         send_pre(t).start()
 
-    for b in range(ff // 128):
-        lane = slice(b * 128, b * 128 + 128)
-        rfcol[lane, :] = jnp.broadcast_to(rf[0:1, lane], (128, 128)).T
+    colacc[...] = jnp.zeros_like(colacc)
 
     for k in range(groups):
         q = lax.rem(lax.div(e, g) + k, groups)
@@ -139,7 +138,7 @@
         for c in range(2 if packed else 1):
             wide = half if packed else ff
             span = slice(c * wide, c * wide + wide)
-            bk = dot(dy, wv[span, :], 1, 1)
+            bk = dot(dy, wv[:, span])
             keep = pre_all[t, :, span].astype(F32) > 0.0
             bk = jnp.where(keep, bk, 0.0).astype(BF16)
             snd[t, :, :, span] = dot(qt[0], bk).reshape(n_e, 8, wide).astype(BF16)
@@ -164,33 +163,33 @@
         back(t)
         loop(n_e, lambda k: send_ret(t, lax.rem(e + n_e // 2 + k, n_e)).start())
 
-    def gradient(c, carry):
-        col, weighted = carry
+    def gradient(c):
         span = pl.ds(pl.multiple_of(c * chunk, 128), chunk)
         acc = None
         for t in range(n_dp):
-            hidden = jnp.maximum(pre_all[t, :, span], 0)
-            part = dot(hidden, dyn[t], 0, 0)
+            part = dot(dyn[t], jnp.maximum(pre_all[t, :, span], 0), 0, 0)
             acc = part if acc is None else acc + part
-        grad[span, :] = acc
+        grad[:, span] = acc
         sq = acc * acc
-        rn = 0.8 * rfcol[span, 0:1] + 0.2 * (jnp.sum(sq, axis=1, keepdims=True) / d + 1e-30)
-        rncol[span, :] = jnp.broadcast_to(rn, (chunk, 128))
-        return (col + jnp.sum(sq, axis=0, keepdims=True),
-                weighted + jnp.sum(sq * (1.0 / rn), axis=0, keepdims=True))
-
-    zero = jnp.zeros((1, d), F32)
-    col, weighted = lax.fori_loop(0, ff // chunk, gradient, (zero, zero))
-    colst[i, 0:1, :] = col
-    colst[i, 1:2, :] = weighted
+        rn = 0.8 * rf[0:1, span] + 0.2 * (jnp.sum(sq, axis=0, keepdims=True) / d + 1e-30)
+        newrow[0:1, span] = rn
+        for k, x in enumerate((sq, sq * (1.0 / rn))):
+            folded = x[:, 0:128]
+            for b in range(1, chunk // 128):
+                folded = folded + x[:, b * 128:b * 128 + 128]
+            colacc[k, 0:d, :] += folded
+
+    loop(ff // chunk, gradient)
+    blocks = [(b, min(b + 128, d)) for b in range(0, d, 128)]
+    for k in range(2):
+        for lo, hi in blocks:
+            sums = jnp.sum(colacc[k, lo:lo + 128, :].T, axis=0, keepdims=True)
+            colst[i, k:k + 1, lo:hi] = sums[:, 0:hi - lo]
     for t in others:
         send_st(t).start()
-    for b in range(ff // 128):
-        lane = slice(b * 128, b * 128 + 128)
-        newrow[0:1, lane] = rncol[lane, :].T[0:1, :]
     for t in others:
         pltpu.make_async_copy(colst.at[i], colst.at[t], st_r.at[t]).wait()
-    col, weighted = zero, zero
+    col, weighted = jnp.zeros((1, d), F32), jnp.zeros((1, d), F32)
     for t in range(n_dp):
         col = col + colst[t, 0:1, :]
         weighted = weighted + colst[t, 1:2, :]
@@ -198,19 +197,17 @@
     cn = 0.8 * cf[...] + 0.2 * (col / full + 1e-30)
     newcol[...] = cn
     spread = jnp.sqrt(jnp.sum(weighted / cn, axis=1, keepdims=True) / (full * d))
-    cs = lax.rsqrt(cn) / jnp.maximum(1.0, spread / 0.01)
-
-    def write(c):
-        span = pl.ds(pl.multiple_of(c * chunk, 128), chunk)
-        return pltpu.make_async_copy(wv.at[span, :], neww.at[0, span, :], outs.at[c])
+    cspad[...] = jnp.zeros_like(cspad)
+    cspad[0:1, 0:d] = lax.rsqrt(cn) / jnp.maximum(1.0, spread / 0.01)
+    for lo, hi in blocks:
+        cscol[lo:lo + 128, :] = jnp.broadcast_to(cspad[0:1, lo:lo + 128], (128, 128)).T
 
     def apply(c):
-        span = pl.ds(pl.multiple_of(c * chunk, 128), chunk)
-        update = grad[span, :] * lax.rsqrt(rncol[span, 0:1]) * cs
-        wv[span, :] = (wv[span, :].astype(F32) - update).astype(BF16)
-        write(c).start()
-
-    loop(ff // chunk, apply)
+        span = pl.ds(pl.multiple_of(c * deep, 16), deep)
+        update = grad[span, :] * lax.rsqrt(newrow[...]) * cscol[span, 0:1]
+        neww[0, span, :] = (wv[span, :].astype(F32) - update).astype(BF16)
+
+    loop(d // deep, apply)
 
     for t in [i] + others:
         loop(n_e, lambda j: pltpu.make_async_copy(
@@ -230,7 +227,15 @@
             send_fw(t, q).wait_send()
         loop(n_e, lambda k: send_ret(t, k).wait_send())
         send_st(t).wait_send()
-    loop(ff // chunk, lambda c: write(c).wait())
+
+
+def flush(a, b, c, d, ao, bo, co, do, sem):
+    pairs = ((b, bo), (a, ao), (c, co), (d, do))
+    copies = [pltpu.make_async_copy(x, y, sem.at[k]) for k, (x, y) in enumerate(pairs)]
+    for copy in copies:
+        copy.start()
+    for copy in copies:
+        copy.wait()
 
 
 def shards(out_grad, routes, pre_act, out_weight, row_factor, col_factor):
@@ -244,6 +249,7 @@
     kinds = 3 if packed else 1
     groups = 4
     chunk = next(c for c in (384, 256, 128) if ff % c == 0)
+    deep = max(c for c in range(16, 257, 16) if d % c == 0)
     wide_d = up128(d) + d - d // 2 // 128 * 128 if packed else d
     wide_f = ff + ff // 2 if packed else ff
     row = np.arange(r)
@@ -259,33 +265,45 @@
     vm = pl.BlockSpec(memory_space=pltpu.VMEM)
     hbm = pl.BlockSpec(memory_space=pl.ANY)
     dma = pltpu.SemaphoreType.DMA
-    sds = jax.ShapeDtypeStruct
-    return pl.pallas_call(
-        functools.partial(kernel, (n_dp, n_e, slot, groups, chunk)),
-        out_shape=(sds((tok, ff * n_dp), BF16), sds((1, ff, d), BF16),
-                   sds((1, ff), F32), sds((1, d), F32)),
-        in_specs=[vm, vm, vm, hbm, hbm, vm, vm, vm, vm],
-        out_specs=(vm, hbm, vm, vm),
+    out = pltpu.VMEM
+    hid, neww, newrow, newcol = pl.pallas_call(
+        functools.partial(kernel, (n_dp, n_e, slot, groups, chunk, deep)),
+        out_shape=(out((tok, ff * n_dp), BF16), out((1, d, ff), BF16),
+                   out((1, ff), F32), out((1, d), F32)),
+        in_specs=[vm, vm, hbm, hbm, vm, vm, vm, vm],
+        out_specs=(vm, vm, vm, vm),
         scratch_shapes=[
             pltpu.VMEM((n_e, 8, wide_d), BF16),
             pltpu.VMEM((n_dp, n_e, 8, wide_d), BF16),
             pltpu.VMEM((n_dp, r, d), BF16),
             pltpu.VMEM((n_dp, r, ff), BF16),
-            pltpu.VMEM((ff, d), BF16),
-            pltpu.VMEM((ff, d), F32),
+            pltpu.VMEM((d, ff), BF16),
+            pltpu.VMEM((d, ff), F32),
             pltpu.VMEM((n_dp, n_e, 8, wide_f), BF16),
             pltpu.VMEM((n_dp, n_e, 8, wide_f), BF16),
             pltpu.VMEM((n_dp, 2, d), F32),
             pltpu.VMEM((kinds, n_e * 8, tok), BF16),
-            pltpu.VMEM((ff, 128), F32),
-            pltpu.VMEM((ff, 128), F32),
-            dma((2,)), dma((ff // chunk,)), dma((n_e,)), dma((n_e,)),
+            pltpu.VMEM((2, up128(d), 128), F32),
+            pltpu.VMEM((1, up128(d)), F32),
+            pltpu.VMEM((up128(d), 128), F32),
+            dma((2,)), dma((n_e,)), dma((n_e,)),
             dma((n_dp, groups)), dma((n_dp, groups)), dma((n_dp,)), dma((n_dp,)),
             dma((n_dp, n_e)), dma((n_dp, n_e)), dma((n_dp,)), dma((n_dp,)),
         ],
         compiler_params=pltpu.CompilerParams(
-            collective_id=0, has_side_effects=True, vmem_limit_bytes=60 * 1024 * 1024),
-    )(out_grad, routes, routes.reshape(1, tok), pre_act, out_weight, row_factor, col_factor, qn, qt)
+            collective_id=0, has_side_effects=True, vmem_limit_bytes=59 * 1024 * 1024),
+    )(out_grad.T, routes.reshape(1, tok), pre_act, jnp.swapaxes(out_weight, 1, 2), row_factor,
+      col_factor, qn, qt)
+    held = (hid, neww, newrow, newcol)
+    hid, neww, newrow, newcol = pl.pallas_call(
+        flush,
+        out_shape=tuple(jax.ShapeDtypeStruct(x.shape, x.dtype) for x in held),
+        in_specs=[vm] * 4,
+        out_specs=[hbm] * 4,
+        scratch_shapes=[dma((4,))],
+        compiler_params=pltpu.CompilerParams(vmem_limit_bytes=1024 * 1024),
+    )(*held)
+    return hid, jnp.swapaxes(neww, 1, 2), newrow, newcol
 
 
 def solution(mesh):

time: 71.8 us -> 55.8 us (0.78)
  local copies, waits for them, and re-layouts: 16.4 us -> 0 us
    unnamed x12 -> x0, local copies, waits for them, and re-layouts: 10.7 us -> none
    pallas_call x1 -> x0, local copies, waits for them, and re-layouts: 5.7 us -> none  [shards(): pl.pallas_call(functools.partial(kernel, (n_dp, n_e, slot, groups, chunk)...]
    pallas_call x1 -> x2, Pallas kernels: 54.3 us -> 55 us  [the longest x1 53.1 us: shards(): pl.pallas_call(functools.partial(kernel, (n_dp, n_e, slot, groups, chunk,...]
where the time goes in v2:
time: 55.8 us; the launch traced here: 55.7 us
  Pallas kernels  55 us (99%)
  between operations  0.64 us (1%)
    pallas_call x1, Pallas kernels, shards(): pl.pallas_call(functools.partial(kernel, (n_dp, n_e, slot, groups, chunk,...  53.1 us
    pallas_call x1, Pallas kernels, shards(): pl.pallas_call(flush, out_shape=tuple((jax.ShapeDtypeStruct(x.shape, x.dt...  1.97 us

profile of v2, /device:TPU:0, one launch (start us, length us, event | category | flops | bytes accessed | tf_op | source)
XLA Modules:
  0.0 55.7 jit_solution(5202199230772469088)
XLA Ops:
  0.6 53.1 %shard_map.111 = (bf16[128,3072]{1,0:T(8,128)(2,1)S(1)}, bf16[1,1040,1536]{2,1,0:T(8,128)(2,1)S(1)}, f32[1,1536]{1,0:T(1,128)S(1)}, f32[1,1040]{1,0:T(1,128)S(1)}) custom-call(bf16[1040,128]{1,0:T(8,128)(2,1)} %bitcast.5, s32[1,128]{1,0:T(1,128)} %bitcast.6, bf16[192,3072]{1,0:T(8,128)(2,1)} %pre.1, bf16[1,1040,1536]{2,1,0:T(8,128)(2,1)} %bitcast.4, ...), custom_call_target="tpu_custom_call" | custom-call | tf_op jit(solution)/shard_map/pallas_call | solution.py:269
  53.7 2.0 %shard_map.112 = (bf16[128,3072]{1,0:T(8,128)(2,1)}, bf16[1,1040,1536]{2,1,0:T(8,128)(2,1)}, f32[1,1536]{1,0:T(1,128)}, f32[1,1040]{1,0:T(1,128)}) custom-call(bf16[128,3072]{1,0:T(8,128)(2,1)S(1)} %get-tuple-element.12.a, bf16[1,1040,1536]{2,1,0:T(8,128)(2,1)S(1)} %get-tuple-element.13.b, f32[1,1536]{1,0:T(1,128)S(1)} %get-tuple-element.14.c, ...), custom_call_target="tpu_custom_call" | custom-call | tf_op jit(solution)/shard_map/pallas_call | solution.py:298

commit v3 on v2

--- a/solution.py
+++ b/solution.py
@@ -33,7 +33,7 @@
     r = pre.shape[0]
     packed = slot > 8
     half, dp_off, h0 = ff // 2, up128(d), d // 2 // 128 * 128
-    hw = d - h0
+    rest = d - 2 * h0
     g = n_e // groups
     i, e = lax.axis_index("dp"), lax.axis_index("expert")
     total = n_dp * n_e
@@ -68,8 +68,11 @@
     if packed:
         place[1] = onehot(rows == jnp.where(order >= 8.0, base - 8.0, -1.0))
         place[2] = onehot(rows == jnp.where(order >= 8.0, base - 4.0, -1.0))
-        tail = dot(place[1], og[0:hw, :], 1, 1) + dot(place[2], og[h0:d, :], 1, 1)
-        dy_out[:, :, dp_off:dp_off + hw] = tail.reshape(n_e, 8, hw).astype(BF16)
+        tail = dot(place[1], og[0:h0, :], 1, 1) + dot(place[2], og[h0:2 * h0, :], 1, 1)
+        dy_out[:, :, dp_off:dp_off + h0] = tail.reshape(n_e, 8, h0).astype(BF16)
+        if rest:
+            more = dot(place[1], og[2 * h0:d, :], 1, 1)
+            dy_out[:, :, d:d + rest] = more.reshape(n_e, 8, rest).astype(BF16)
 
     def peer(k):
         return lax.rem(e + lax.rem(k + n_e // 2 - 1, n_e - 1) + 1, n_e)
@@ -100,6 +103,9 @@
         return pltpu.make_async_remote_copy(
             src_ref=colst.at[i], dst_ref=colst.at[i], send_sem=st_s.at[t],
             recv_sem=st_r.at[i], device_id=(t, e), device_id_type=MESH)
+
+    near = lax.div(e, n_e // 2)
+    far = 1 - near
 
     def loop(n, act):
         def step(k, _):
@@ -108,16 +114,16 @@
         lax.fori_loop(0, n, step, 0)
 
     pl.semaphore_wait(barrier, total - 1)
+    for t in others:
+        send_pre(t).start()
     loop(n_e - 1, lambda k: send_dy(k).start())
     own = pltpu.make_async_copy(dy_out.at[e], dy_all.at[i, e], dy_r.at[e])
     own.start()
-    for t in others:
-        send_pre(t).start()
 
     colacc[...] = jnp.zeros_like(colacc)
 
     for k in range(groups):
-        q = lax.rem(lax.div(e, g) + k, groups)
+        q = lax.rem(far * (groups // 2) + k, groups)
         for m in range(g):
             j = q * g + m
             pltpu.make_async_copy(dy_out.at[0], dy_all.at[i, j], dy_r.at[j]).wait()
@@ -127,41 +133,57 @@
     def flat_rows(x):
         return x.astype(F32).reshape(x.shape[0] * 8, x.shape[2]).astype(BF16)
 
-    def back(t):
-        dy = dot(qn[0], flat_rows(dy_all[t, :, :, 0:d]))
+    def back(t, first, count):
+        n = count * slot
+        part = pl.ds(first, count)
+        where = pl.ds(first * slot if isinstance(first, int) else pl.multiple_of(first * slot, 16), n)
+        dy = dot(qn[0, 0:n, 0:count * 8], flat_rows(dy_all[t, part, :, 0:d]))
         if packed:
-            tail = flat_rows(dy_all[t, :, :, dp_off:dp_off + hw])
-            dy = dy + jnp.concatenate([dot(qn[1], tail[:, 0:h0]), dot(qn[2], tail)], axis=1)
+            q_lo, q_hi = qn[1, 0:n, 0:count * 8], qn[2, 0:n, 0:count * 8]
+            tail = flat_rows(dy_all[t, part, :, dp_off:dp_off + h0])
+            pieces = [dot(q_lo, tail), dot(q_hi, tail)]
+            if rest:
+                ends = dot(q_lo, flat_rows(dy_all[t, part, :, 2 * h0:dp_off]))
+                pieces.append(ends[:, d - 2 * h0:d - 2 * h0 + rest])
+            dy = dy + jnp.concatenate(pieces, axis=1)
         dy = dy.astype(BF16)
-        dyn[t] = dy
+        dyn[t, where, :] = dy
         tail = None
         for c in range(2 if packed else 1):
             wide = half if packed else ff
             span = slice(c * wide, c * wide + wide)
             bk = dot(dy, wv[:, span])
-            keep = pre_all[t, :, span].astype(F32) > 0.0
+            keep = pre_all[t, where, span].astype(F32) > 0.0
             bk = jnp.where(keep, bk, 0.0).astype(BF16)
-            snd[t, :, :, span] = dot(qt[0], bk).reshape(n_e, 8, wide).astype(BF16)
+            snd[t, part, :, span] = dot(qt[0, 0:count * 8, 0:n], bk).reshape(count, 8, wide).astype(BF16)
             if packed:
-                part = dot(qt[1 + c], bk)
-                tail = part if tail is None else tail + part
+                more = dot(qt[1 + c, 0:count * 8, 0:n], bk)
+                tail = more if tail is None else tail + more
         if packed:
-            snd[t, :, :, ff:ff + half] = tail.reshape(n_e, 8, half).astype(BF16)
+            snd[t, part, :, ff:ff + half] = tail.reshape(count, 8, half).astype(BF16)
 
     get_w.wait()
     get_pre.wait()
-    back(i)
+    back(i, 0, n_e)
     loop(n_e - 1, lambda k: send_ret(i, peer(k)).start())
     own_ret = pltpu.make_async_copy(snd.at[i, e], ret.at[i, e], rt_r.at[i, e])
     own_ret.start()
 
-    for t in others:
-        for q in range(groups):
-            part = pl.ds(q * g, g)
-            pltpu.make_async_copy(dy_all.at[i, part], dy_all.at[t, part], fw_r.at[t, q]).wait()
+    side = n_e // 2
+
+    def send_side(t, which):
+        loop(side, lambda k: send_ret(t, which * side + lax.rem(e + k, side)).start())
+
+    for t in others:
         pltpu.make_async_copy(pre_all.at[i], pre_all.at[t], pre_r.at[t]).wait()
-        back(t)
-        loop(n_e, lambda k: send_ret(t, lax.rem(e + n_e // 2 + k, n_e)).start())
+        for which in (far, near):
+            for k in range(groups // 2):
+                q = which * (groups // 2) + k
+                part = pl.ds(q * g, g)
+                pltpu.make_async_copy(dy_all.at[i, part], dy_all.at[t, part], fw_r.at[t, q]).wait()
+            back(t, which * side, side)
+            if which is far:
+                send_side(t, far)
 
     def gradient(c):
         span = pl.ds(pl.multiple_of(c * chunk, 128), chunk)
@@ -187,6 +209,7 @@
             colst[i, k:k + 1, lo:hi] = sums[:, 0:hi - lo]
     for t in others:
         send_st(t).start()
+        send_side(t, near)
     for t in others:
         pltpu.make_async_copy(colst.at[i], colst.at[t], st_r.at[t]).wait()
     col, weighted = jnp.zeros((1, d), F32), jnp.zeros((1, d), F32)
@@ -250,7 +273,8 @@
     groups = 4
     chunk = next(c for c in (384, 256, 128) if ff % c == 0)
     deep = max(c for c in range(16, 257, 16) if d % c == 0)
-    wide_d = up128(d) + d - d // 2 // 128 * 128 if packed else d
+    wide_d = up128(d) + d // 2 // 128 * 128 if packed else d
+    assert not packed or 2 * d - d // 256 * 256 <= up128(d)
     wide_f = ff + ff // 2 if packed else ff
     row = np.arange(r)
     src, s = row // slot, row % slot

time: 55.8 us -> 54.4 us (0.975)
  Pallas kernels: 55 us -> 53.6 us
    pallas_call x1, Pallas kernels: 53.1 us -> 51.6 us  [shards(): pl.pallas_call(functools.partial(kernel, (n_dp, n_e, slot, groups, chunk,...]
where the time goes in v3:
time: 54.4 us; the launch traced here: 54.2 us
  Pallas kernels  53.6 us (99%)
  between operations  0.64 us (1%)
    pallas_call x1, Pallas kernels, shards(): pl.pallas_call(functools.partial(kernel, (n_dp, n_e, slot, groups, chunk,...  51.6 us
    pallas_call x1, Pallas kernels, shards(): pl.pallas_call(flush, out_shape=tuple((jax.ShapeDtypeStruct(x.shape, x.dt...  1.97 us

profile of v3, /device:TPU:0, one launch (start us, length us, event | category | flops | bytes accessed | tf_op | source)
XLA Modules:
  0.0 54.2 jit_solution(1854596194811611357)
XLA Ops:
  0.6 51.6 %shard_map.111 = (bf16[128,3072]{1,0:T(8,128)(2,1)S(1)}, bf16[1,1040,1536]{2,1,0:T(8,128)(2,1)S(1)}, f32[1,1536]{1,0:T(1,128)S(1)}, f32[1,1040]{1,0:T(1,128)S(1)}) custom-call(bf16[1040,128]{1,0:T(8,128)(2,1)} %bitcast.5, s32[1,128]{1,0:T(1,128)} %bitcast.6, bf16[192,3072]{1,0:T(8,128)(2,1)} %pre.1, bf16[1,1040,1536]{2,1,0:T(8,128)(2,1)} %bitcast.4, ...), custom_call_target="tpu_custom_call" | custom-call | tf_op jit(solution)/shard_map/pallas_call | solution.py:293
  52.2 2.0 %shard_map.112 = (bf16[128,3072]{1,0:T(8,128)(2,1)}, bf16[1,1040,1536]{2,1,0:T(8,128)(2,1)}, f32[1,1536]{1,0:T(1,128)}, f32[1,1040]{1,0:T(1,128)}) custom-call(bf16[128,3072]{1,0:T(8,128)(2,1)S(1)} %get-tuple-element.12.a, bf16[1,1040,1536]{2,1,0:T(8,128)(2,1)S(1)} %get-tuple-element.13.b, f32[1,1536]{1,0:T(1,128)S(1)} %get-tuple-element.14.c, ...), custom_call_target="tpu_custom_call" | custom-call | tf_op jit(solution)/shard_map/pallas_call | solution.py:322

commit v4 on v3

--- a/solution.py
+++ b/solution.py
@@ -74,11 +74,14 @@
             more = dot(place[1], og[2 * h0:d, :], 1, 1)
             dy_out[:, :, d:d + rest] = more.reshape(n_e, 8, rest).astype(BF16)
 
-    def peer(k):
-        return lax.rem(e + lax.rem(k + n_e // 2 - 1, n_e - 1) + 1, n_e)
-
-    def send_dy(k):
-        t = peer(k)
+    side = n_e // 2
+    near = lax.div(e, side)
+    far = 1 - near
+
+    def over(which, k):
+        return which * side + lax.rem(e + k, side)
+
+    def send_dy(t):
         return pltpu.make_async_remote_copy(
             src_ref=dy_out.at[t], dst_ref=dy_all.at[i, e], send_sem=dy_s.at[t],
             recv_sem=dy_r.at[e], device_id=(i, t), device_id_type=MESH)
@@ -103,9 +106,6 @@
         return pltpu.make_async_remote_copy(
             src_ref=colst.at[i], dst_ref=colst.at[i], send_sem=st_s.at[t],
             recv_sem=st_r.at[i], device_id=(t, e), device_id_type=MESH)
-
-    near = lax.div(e, n_e // 2)
-    far = 1 - near
 
     def loop(n, act):
         def step(k, _):
@@ -113,22 +113,27 @@
             return 0
         lax.fori_loop(0, n, step, 0)
 
+    def all_peers(act):
+        loop(side, lambda k: act(over(far, k)))
+        loop(side - 1, lambda k: act(over(near, k + 1)))
+
     pl.semaphore_wait(barrier, total - 1)
     for t in others:
         send_pre(t).start()
-    loop(n_e - 1, lambda k: send_dy(k).start())
+    all_peers(lambda t: send_dy(t).start())
     own = pltpu.make_async_copy(dy_out.at[e], dy_all.at[i, e], dy_r.at[e])
     own.start()
 
     colacc[...] = jnp.zeros_like(colacc)
 
-    for k in range(groups):
-        q = lax.rem(far * (groups // 2) + k, groups)
-        for m in range(g):
-            j = q * g + m
-            pltpu.make_async_copy(dy_out.at[0], dy_all.at[i, j], dy_r.at[j]).wait()
-        for t in others:
-            send_fw(t, q).start()
+    def receive(which):
+        for k in range(groups // 2):
+            q = which * (groups // 2) + k
+            for m in range(g):
+                j = q * g + m
+                pltpu.make_async_copy(dy_out.at[0], dy_all.at[i, j], dy_r.at[j]).wait()
+            for t in others:
+                send_fw(t, q).start()
 
     def flat_rows(x):
         return x.astype(F32).reshape(x.shape[0] * 8, x.shape[2]).astype(BF16)
@@ -162,17 +167,19 @@
         if packed:
             snd[t, part, :, ff:ff + half] = tail.reshape(count, 8, half).astype(BF16)
 
+    receive(far)
     get_w.wait()
     get_pre.wait()
-    back(i, 0, n_e)
-    loop(n_e - 1, lambda k: send_ret(i, peer(k)).start())
+    back(i, far * side, side)
+    loop(side, lambda k: send_ret(i, over(far, k)).start())
+    receive(near)
+    back(i, near * side, side)
+    loop(side - 1, lambda k: send_ret(i, over(near, k + 1)).start())
     own_ret = pltpu.make_async_copy(snd.at[i, e], ret.at[i, e], rt_r.at[i, e])
     own_ret.start()
 
-    side = n_e // 2
-
     def send_side(t, which):
-        loop(side, lambda k: send_ret(t, which * side + lax.rem(e + k, side)).start())
+        loop(side, lambda k: send_ret(t, over(which, k)).start())
 
     for t in others:
         pltpu.make_async_copy(pre_all.at[i], pre_all.at[t], pre_r.at[t]).wait()
@@ -242,8 +249,8 @@
                 got = got + dot(place[1 + c], flat_rows(ret[t, :, :, ff:ff + half]), 0, 0)
             hid[:, pl.ds(pl.multiple_of(t * ff + c * wide, 128), wide)] = got.astype(BF16)
 
-    loop(n_e - 1, lambda k: send_dy(k).wait_send())
-    loop(n_e - 1, lambda k: send_ret(i, peer(k)).wait_send())
+    all_peers(lambda t: send_dy(t).wait_send())
+    all_peers(lambda t: send_ret(i, t).wait_send())
     for t in others:
         send_pre(t).wait_send()
         for q in range(groups):

time: 54.4 us -> 53.6 us (0.985)
  Pallas kernels: 53.6 us -> 52.8 us
    pallas_call x1, Pallas kernels: 51.6 us -> 50.9 us  [shards(): pl.pallas_call(functools.partial(kernel, (n_dp, n_e, slot, groups, chunk,...]
where the time goes in v4:
time: 53.6 us; the launch traced here: 53.5 us
  Pallas kernels  52.8 us (99%)
  between operations  0.64 us (1%)
    pallas_call x1, Pallas kernels, shards(): pl.pallas_call(functools.partial(kernel, (n_dp, n_e, slot, groups, chunk,...  50.9 us
    pallas_call x1, Pallas kernels, shards(): pl.pallas_call(flush, out_shape=tuple((jax.ShapeDtypeStruct(x.shape, x.dt...  1.97 us

profile of v4, /device:TPU:0, one launch (start us, length us, event | category | flops | bytes accessed | tf_op | source)
XLA Modules:
  0.0 53.5 jit_solution(7569420222657812416)
XLA Ops:
  0.6 50.9 %shard_map.111 = (bf16[128,3072]{1,0:T(8,128)(2,1)S(1)}, bf16[1,1040,1536]{2,1,0:T(8,128)(2,1)S(1)}, f32[1,1536]{1,0:T(1,128)S(1)}, f32[1,1040]{1,0:T(1,128)S(1)}) custom-call(bf16[1040,128]{1,0:T(8,128)(2,1)} %bitcast.5, s32[1,128]{1,0:T(1,128)} %bitcast.6, bf16[192,3072]{1,0:T(8,128)(2,1)} %pre.1, bf16[1,1040,1536]{2,1,0:T(8,128)(2,1)} %bitcast.4, ...), custom_call_target="tpu_custom_call" | custom-call | tf_op jit(solution)/shard_map/pallas_call | solution.py:300
  51.5 2.0 %shard_map.112 = (bf16[128,3072]{1,0:T(8,128)(2,1)}, bf16[1,1040,1536]{2,1,0:T(8,128)(2,1)}, f32[1,1536]{1,0:T(1,128)}, f32[1,1040]{1,0:T(1,128)}) custom-call(bf16[128,3072]{1,0:T(8,128)(2,1)S(1)} %get-tuple-element.12.a, bf16[1,1040,1536]{2,1,0:T(8,128)(2,1)S(1)} %get-tuple-element.13.b, f32[1,1536]{1,0:T(1,128)S(1)} %get-tuple-element.14.c, ...), custom_call_target="tpu_custom_call" | custom-call | tf_op jit(solution)/shard_map/pallas_call | solution.py:329
